TPU v7x, 256 devices: a whole 4x4x8 slice. The times are simulated.
256 devices in a mesh: blk: 8 (over x_hi, y), group: 32 (over z, x_lo, core).
Axes of the slice: x: 4 (x_hi: 2, x_lo: 2; x = x_hi * 2 + x_lo), y: 4, z: 8, core: 2. Of those that a mesh axis runs over, the one named last changes fastest.
Arguments:
- walk_rows: bfloat16 [4096, 131072], P('blk', 'group'), may hold values from -6 to 6
- col_values: bfloat16 [49152, 4096], P('group', 'blk'), may hold values from -0.02734375 to 0.02734375
- col_index: int32 [96, 8], P('group'), may hold values from 0 to 7
- col_count: int32 [32, 8], P('group'), may hold values from 1 to 3, as said below
Outputs:
- inflated: float32 [4096, 4096], P(('blk', 'group'))
Inputs may be any that keep to these rules, and one draw needn't show every extreme that they name: `col_count`: each list holds 1 to 3 valid slots; some list holds 3; contents of the other slots are arbitrary.
All inputs are finite; a program needn't handle non-finite values.
Results may differ from a plain program's by a relative error of at most 0.0003.
Values may be sent and summed in bfloat16 or wider, within the bound.
No kernel may reach another device: no remote copies, remote signals or barrier semaphores. Data moves between devices by JAX's collectives and lax.ppermute only.
A program may use at most 64 MiB of HBM per device.

v0:
```python
import jax
import jax.numpy as jnp
from jax import lax
from jax.sharding import PartitionSpec as P


def shifted(shard, axis, by):
    size = lax.axis_size(axis)
    return lax.ppermute(shard, axis, [(i, (i + by) % size) for i in range(size)])


def on_device(walk_rows, col_values, col_index, col_count):
    width = col_values.shape[1]
    slots = col_values.shape[0] // width
    nblock = lax.axis_size("blk")
    myself = lax.axis_index("blk")
    rows_here = walk_rows.shape[0]
    share = rows_here // lax.axis_size("group")

    def panel_product(rows, values, panel):
        index = lax.dynamic_slice_in_dim(col_index, panel, 1, 1)[:, 0]
        count = lax.dynamic_slice_in_dim(col_count, panel, 1, 1)[0, 0]
        total = jnp.zeros((rows.shape[0], width), jnp.float32)
        for slot in range(slots):
            block = lax.dynamic_slice_in_dim(rows, index[slot] * width, width, 1)
            piece = values[slot * width : (slot + 1) * width]
            product = jnp.dot(block, piece, preferred_element_type=jnp.float32)
            total = total + jnp.where(slot < count, product, jnp.zeros_like(product))
        return total

    def turn(step, carry):
        values, result = carry
        panel = (myself - step) % nblock
        part = panel_product(walk_rows, values, panel)
        reduced = lax.psum_scatter(part, "group", scatter_dimension=0, tiled=True)
        result = lax.dynamic_update_slice_in_dim(result, reduced, panel * width, 1)
        values = shifted(values, "blk", 1)
        return (values, result)

    start_out = jnp.zeros((share, nblock * width), jnp.float32)
    unused, expanded = lax.fori_loop(0, nblock, turn, (col_values, start_out))
    squared = expanded * expanded
    column = jnp.sum(squared, axis=0)
    total = lax.psum(column, ("blk", "group"))
    scale = total / (nblock * rows_here) + 1e-06
    return squared / scale


def solution(mesh):
    return jax.shard_map(
        on_device,
        mesh=mesh,
        in_specs=(P("blk", "group"), P("group", "blk"), P("group", None), P("group", None)),
        out_specs=P(("blk", "group"), None),
        check_vma=False,
    )
```

profile of v0, /device:TPU:1, one launch (start us, length us, event | category | flops | bytes accessed | tf_op | source)
XLA Modules:
  0.0 1125.3 jit_solution(7067308069750690020)
XLA Ops:
  6.6 1.4 copy-done
  7.9 1030.1 %while.17 = (s32[]{:T(128)}, bf16[1536,512]{1,0:T(8,128)(2,1)S(1)}, f32[16,4096]{1,0:T(8,128)S(1)}, s32[]{:T(128)}, s32[1,8]{1,0:T(1,128)S(1)}, /*index=5*/s32[3...) while((s32[]{:T(128)}, bf16[1536,512]{1,0:T(8,128)(2,1)S(1)}, ...), condition=%wide.region_2.3_spmd, body=%wide.region_0.2_spmd.sunk | while | flops 806617088 | bytes 21137560 | solution.py:41
  10.5 0.7 fusion.29
  12.4 2.1 convolution_select_fusion.5
  14.5 1.5 convolution_select_fusion.6
  16.0 2.5 fusion.30
  18.5 2.2 collective-permute-start
  20.7 117.8 %reduce-scatter.2.cloned.1.call-done = f32[16,512]{1,0:T(8,128)} async-done(((f32[512,512]{1,0:T(8,128)}), f32[16,512]{1,0:T(8,128)}) %reduce-scatter.2.cloned.1.call-update) | async-done | bytes 32784 | tf_op jit(solution)/shard_map/while/body/eval_jaxpr/reduce_scatter | solution.py:35
  138.5 0.8 constant_dynamic-update-slice_fusion.2
  143.7 2.1 convolution_select_fusion.5
  145.8 1.5 convolution_select_fusion.6
  147.3 2.5 fusion.30
  149.9 117.1 %reduce-scatter.2.cloned.1.call-done = f32[16,512]{1,0:T(8,128)} async-done(((f32[512,512]{1,0:T(8,128)}), f32[16,512]{1,0:T(8,128)}) %reduce-scatter.2.cloned.1.call-update) | async-done | bytes 32784 | tf_op jit(solution)/shard_map/while/body/eval_jaxpr/reduce_scatter | solution.py:35
  267.0 0.8 constant_dynamic-update-slice_fusion.2
  272.2 2.1 convolution_select_fusion.5
  274.3 1.5 convolution_select_fusion.6
  275.8 2.5 fusion.30
  278.4 116.7 %reduce-scatter.2.cloned.1.call-done = f32[16,512]{1,0:T(8,128)} async-done(((f32[512,512]{1,0:T(8,128)}), f32[16,512]{1,0:T(8,128)}) %reduce-scatter.2.cloned.1.call-update) | async-done | bytes 32784 | tf_op jit(solution)/shard_map/while/body/eval_jaxpr/reduce_scatter | solution.py:35
  395.1 0.8 constant_dynamic-update-slice_fusion.2
  400.4 2.1 convolution_select_fusion.5
  402.5 1.5 convolution_select_fusion.6
  404.0 2.5 fusion.30
  406.6 116.8 %reduce-scatter.2.cloned.1.call-done = f32[16,512]{1,0:T(8,128)} async-done(((f32[512,512]{1,0:T(8,128)}), f32[16,512]{1,0:T(8,128)}) %reduce-scatter.2.cloned.1.call-update) | async-done | bytes 32784 | tf_op jit(solution)/shard_map/while/body/eval_jaxpr/reduce_scatter | solution.py:35
  523.4 0.8 constant_dynamic-update-slice_fusion.2
  526.8 0.7 fusion.29
  528.7 2.1 convolution_select_fusion.5
  530.8 1.5 convolution_select_fusion.6
  532.3 2.5 fusion.30
  535.0 116.8 %reduce-scatter.2.cloned.1.call-done = f32[16,512]{1,0:T(8,128)} async-done(((f32[512,512]{1,0:T(8,128)}), f32[16,512]{1,0:T(8,128)}) %reduce-scatter.2.cloned.1.call-update) | async-done | bytes 32784 | tf_op jit(solution)/shard_map/while/body/eval_jaxpr/reduce_scatter | solution.py:35
  651.9 0.8 constant_dynamic-update-slice_fusion.2
  657.1 2.1 convolution_select_fusion.5
  659.2 1.5 convolution_select_fusion.6
  660.7 2.5 fusion.30
  663.5 116.9 %reduce-scatter.2.cloned.1.call-done = f32[16,512]{1,0:T(8,128)} async-done(((f32[512,512]{1,0:T(8,128)}), f32[16,512]{1,0:T(8,128)}) %reduce-scatter.2.cloned.1.call-update) | async-done | bytes 32784 | tf_op jit(solution)/shard_map/while/body/eval_jaxpr/reduce_scatter | solution.py:35
  780.3 0.8 constant_dynamic-update-slice_fusion.2
  785.6 2.1 convolution_select_fusion.5
  787.7 1.5 convolution_select_fusion.6
  789.2 2.5 fusion.30
  791.9 116.9 %reduce-scatter.2.cloned.1.call-done = f32[16,512]{1,0:T(8,128)} async-done(((f32[512,512]{1,0:T(8,128)}), f32[16,512]{1,0:T(8,128)}) %reduce-scatter.2.cloned.1.call-update) | async-done | bytes 32784 | tf_op jit(solution)/shard_map/while/body/eval_jaxpr/reduce_scatter | solution.py:35
  908.8 0.8 constant_dynamic-update-slice_fusion.2
  912.1 0.7 fusion.29
  914.0 2.1 convolution_select_fusion.5
  916.1 1.5 convolution_select_fusion.6
  917.6 2.5 fusion.30
  920.6 116.6 %reduce-scatter.2.cloned.1.call-done = f32[16,512]{1,0:T(8,128)} async-done(((f32[512,512]{1,0:T(8,128)}), f32[16,512]{1,0:T(8,128)}) %reduce-scatter.2.cloned.1.call-update) | async-done | bytes 32784 | tf_op jit(solution)/shard_map/while/body/eval_jaxpr/reduce_scatter | solution.py:35
  1037.3 0.8 constant_dynamic-update-slice_fusion.2
  1038.1 79.7 %psum.7 = f32[4096]{0:T(1024)S(1)} all-reduce(f32[4096]{0:T(1024)S(1)} %multiply_reduce_fusion), channel_id=1, replica_groups=mesh['blk'=8,'group'=32] {'blk','group'}, use_global_device_ids=true, to_apply=%region_4.5 | all-reduce | flops 4096 | bytes 32768 | tf_op jit(solution)/shard_map/psum | solution.py:44
  1117.7 0.7 multiply_divide_fusion
  (68 shorter events, 11.2 us)
Async XLA Ops:
  6.5 1.4 copy-start
  6.5 1.4 copy-start.1
  6.5 1.4 copy-start.2
  7.9 130.5 %reduce-scatter.2.cloned.1.call-start = ((), (), s32[]{:S(2)}) async-start(), calls=%async_computation.1 | async-start | bytes 1081344 | tf_op jit(solution)/shard_map/while/body/eval_jaxpr/reduce_scatter | solution.py:35
  18.5 120.8 %collective-permute-start = (bf16[1536,512]{1,0:T(8,128)(2,1)S(1)}, bf16[1536,512]{1,0:T(8,128)(2,1)S(1)}, u32[]{:S(2)}, u32[]{:S(2)}) collective-permute-start(bf16[1536,512]{1,0:T(8,128)(2,1)S(1)} %copy.10), channel_id=1, source_target_pairs={{0,32},{32,64},{64,96},{96,128},{128,160},{160,192},{192,224},{224... | collective-permute-start | bytes 4718600 | tf_op jit(solution)/shard_map/while/body/eval_jaxpr/ppermute | solution.py:9
  139.3 127.7 %reduce-scatter.2.cloned.1.call-start = ((), (), s32[]{:S(2)}) async-start(), calls=%async_computation.1 | async-start | bytes 1081344 | tf_op jit(solution)/shard_map/while/body/eval_jaxpr/reduce_scatter | solution.py:35
  149.8 117.9 %collective-permute-start = (bf16[1536,512]{1,0:T(8,128)(2,1)S(1)}, bf16[1536,512]{1,0:T(8,128)(2,1)S(1)}, u32[]{:S(2)}, u32[]{:S(2)}) collective-permute-start(bf16[1536,512]{1,0:T(8,128)(2,1)S(1)} %copy.10), channel_id=1, source_target_pairs={{0,32},{32,64},{64,96},{96,128},{128,160},{160,192},{192,224},{224... | collective-permute-start | bytes 4718600 | tf_op jit(solution)/shard_map/while/body/eval_jaxpr/ppermute | solution.py:9
  267.7 127.4 %reduce-scatter.2.cloned.1.call-start = ((), (), s32[]{:S(2)}) async-start(), calls=%async_computation.1 | async-start | bytes 1081344 | tf_op jit(solution)/shard_map/while/body/eval_jaxpr/reduce_scatter | solution.py:35
  278.3 117.6 %collective-permute-start = (bf16[1536,512]{1,0:T(8,128)(2,1)S(1)}, bf16[1536,512]{1,0:T(8,128)(2,1)S(1)}, u32[]{:S(2)}, u32[]{:S(2)}) collective-permute-start(bf16[1536,512]{1,0:T(8,128)(2,1)S(1)} %copy.10), channel_id=1, source_target_pairs={{0,32},{32,64},{64,96},{96,128},{128,160},{160,192},{192,224},{224... | collective-permute-start | bytes 4718600 | tf_op jit(solution)/shard_map/while/body/eval_jaxpr/ppermute | solution.py:9
  395.9 127.5 %reduce-scatter.2.cloned.1.call-start = ((), (), s32[]{:S(2)}) async-start(), calls=%async_computation.1 | async-start | bytes 1081344 | tf_op jit(solution)/shard_map/while/body/eval_jaxpr/reduce_scatter | solution.py:35
  406.4 117.8 %collective-permute-start = (bf16[1536,512]{1,0:T(8,128)(2,1)S(1)}, bf16[1536,512]{1,0:T(8,128)(2,1)S(1)}, u32[]{:S(2)}, u32[]{:S(2)}) collective-permute-start(bf16[1536,512]{1,0:T(8,128)(2,1)S(1)} %copy.10), channel_id=1, source_target_pairs={{0,32},{32,64},{64,96},{96,128},{128,160},{160,192},{192,224},{224... | collective-permute-start | bytes 4718600 | tf_op jit(solution)/shard_map/while/body/eval_jaxpr/ppermute | solution.py:9
  524.2 127.7 %reduce-scatter.2.cloned.1.call-start = ((), (), s32[]{:S(2)}) async-start(), calls=%async_computation.1 | async-start | bytes 1081344 | tf_op jit(solution)/shard_map/while/body/eval_jaxpr/reduce_scatter | solution.py:35
  534.8 117.9 %collective-permute-start = (bf16[1536,512]{1,0:T(8,128)(2,1)S(1)}, bf16[1536,512]{1,0:T(8,128)(2,1)S(1)}, u32[]{:S(2)}, u32[]{:S(2)}) collective-permute-start(bf16[1536,512]{1,0:T(8,128)(2,1)S(1)} %copy.10), channel_id=1, source_target_pairs={{0,32},{32,64},{64,96},{96,128},{128,160},{160,192},{192,224},{224... | collective-permute-start | bytes 4718600 | tf_op jit(solution)/shard_map/while/body/eval_jaxpr/ppermute | solution.py:9
  652.6 127.7 %reduce-scatter.2.cloned.1.call-start = ((), (), s32[]{:S(2)}) async-start(), calls=%async_computation.1 | async-start | bytes 1081344 | tf_op jit(solution)/shard_map/while/body/eval_jaxpr/reduce_scatter | solution.py:35
  663.2 117.9 %collective-permute-start = (bf16[1536,512]{1,0:T(8,128)(2,1)S(1)}, bf16[1536,512]{1,0:T(8,128)(2,1)S(1)}, u32[]{:S(2)}, u32[]{:S(2)}) collective-permute-start(bf16[1536,512]{1,0:T(8,128)(2,1)S(1)} %copy.10), channel_id=1, source_target_pairs={{0,32},{32,64},{64,96},{96,128},{128,160},{160,192},{192,224},{224... | collective-permute-start | bytes 4718600 | tf_op jit(solution)/shard_map/while/body/eval_jaxpr/ppermute | solution.py:9
  781.1 127.7 %reduce-scatter.2.cloned.1.call-start = ((), (), s32[]{:S(2)}) async-start(), calls=%async_computation.1 | async-start | bytes 1081344 | tf_op jit(solution)/shard_map/while/body/eval_jaxpr/reduce_scatter | solution.py:35
  791.7 117.9 %collective-permute-start = (bf16[1536,512]{1,0:T(8,128)(2,1)S(1)}, bf16[1536,512]{1,0:T(8,128)(2,1)S(1)}, u32[]{:S(2)}, u32[]{:S(2)}) collective-permute-start(bf16[1536,512]{1,0:T(8,128)(2,1)S(1)} %copy.10), channel_id=1, source_target_pairs={{0,32},{32,64},{64,96},{96,128},{128,160},{160,192},{192,224},{224... | collective-permute-start | bytes 4718600 | tf_op jit(solution)/shard_map/while/body/eval_jaxpr/ppermute | solution.py:9
  909.6 127.7 %reduce-scatter.2.cloned.1.call-start = ((), (), s32[]{:S(2)}) async-start(), calls=%async_computation.1 | async-start | bytes 1081344 | tf_op jit(solution)/shard_map/while/body/eval_jaxpr/reduce_scatter | solution.py:35
  920.1 117.9 %collective-permute-start = (bf16[1536,512]{1,0:T(8,128)(2,1)S(1)}, bf16[1536,512]{1,0:T(8,128)(2,1)S(1)}, u32[]{:S(2)}, u32[]{:S(2)}) collective-permute-start(bf16[1536,512]{1,0:T(8,128)(2,1)S(1)} %copy.10), channel_id=1, source_target_pairs={{0,32},{32,64},{64,96},{96,128},{128,160},{160,192},{192,224},{224... | collective-permute-start | bytes 4718600 | tf_op jit(solution)/shard_map/while/body/eval_jaxpr/ppermute | solution.py:9
Sparse Core Ops, SparseCore 0:
  18.6 119.8 reduce-scatter.1
  149.9 116.9 reduce-scatter.1
  278.4 116.6 reduce-scatter.1
  406.6 116.8 reduce-scatter.1
  534.9 116.9 reduce-scatter.1
  663.3 116.9 reduce-scatter.1
  791.8 116.9 reduce-scatter.1
  920.2 116.9 reduce-scatter.1
where the time goes:
time: 1130 us
  waiting for transfers between devices  936 us (83%)
  blocking collectives  79.7 us (7%)
  matrix products  48.4 us (4%)
  loops' own time  24.6 us (2%)
  local copies, waits for them, and re-layouts  13.6 us (1%)
  between operations  13.4 us (1%)
    reduce_scatter x8, waiting for transfers between devices, turn(): reduced = lax.psum_scatter(part, 'group', scatter_dimension=0, tiled=True)  936 us
    psum x1, blocking collectives, on_device(): total = lax.psum(column, ('blk', 'group'))  79.7 us
    dot_general x24, matrix products, panel_product(): product = jnp.dot(block, piece, preferred_element_type=jnp.float32)  48.4 us
    another operation x1, loops' own time, on_device(): unused, expanded = lax.fori_loop(0, nblock, turn, (col_values, start_out))  24.6 us
  transfers between devices with their start and end apart: 16, of which 8 were waited for; matrix products, arithmetic and copies ran while one was open for 1% of the time, Pallas kernels for 0%

commit v1 on v0

--- a/solution.py
+++ b/solution.py
@@ -41,7 +41,7 @@
     unused, expanded = lax.fori_loop(0, nblock, turn, (col_values, start_out))
     squared = expanded * expanded
     column = jnp.sum(squared, axis=0)
-    total = lax.psum(column, ("blk", "group"))
+    total = jnp.sum(lax.all_gather(column, ("blk", "group")), axis=0)
     scale = total / (nblock * rows_here) + 1e-06
     return squared / scale
 

time: 1130 us -> 1480 us (1.31)
  waiting for transfers between devices: 936 us -> 1360 us
  blocking collectives: 79.7 us -> 0 us
    all_gather x0 -> x1, waiting for transfers between devices: none -> 419 us  [on_device(): total = jnp.sum(lax.all_gather(column, ('blk', 'group')), axis=0)]
    psum x1 -> x0, blocking collectives: 79.7 us -> none  [on_device(): total = lax.psum(column, ('blk', 'group'))]
  transfers between devices with their start and end apart: 16 -> 17, of which waited for: 8 -> 9; matrix products, arithmetic and copies ran while one was open for 1% -> 0% of each run, Pallas kernels for 0% -> 0%
where the time goes in v1:
time: 1480 us
  waiting for transfers between devices  1360 us (92%)
  matrix products  48.3 us (3%)
  loops' own time  26.2 us (2%)
  local copies, waits for them, and re-layouts  18.7 us (1%)
  between operations  14.8 us (1%)
    reduce_scatter x8, waiting for transfers between devices, turn(): reduced = lax.psum_scatter(part, 'group', scatter_dimension=0, tiled=True)  936 us
    all_gather x1, waiting for transfers between devices, on_device(): total = jnp.sum(lax.all_gather(column, ('blk', 'group')), axis=0)  419 us
    dot_general x24, matrix products, panel_product(): product = jnp.dot(block, piece, preferred_element_type=jnp.float32)  48.3 us
  transfers between devices with their start and end apart: 17, of which 9 were waited for; matrix products, arithmetic and copies ran while one was open for 0% of the time, Pallas kernels for 0%

profile of v1, /device:TPU:1, one launch (start us, length us, event | category | flops | bytes accessed | tf_op | source)
XLA Modules:
  0.0 1475.7 jit_solution(11046664849335865723)
XLA Ops:
  7.4 1.4 copy-done
  8.8 1031.8 %while.17 = (s32[]{:T(128)}, bf16[1536,512]{1,0:T(8,128)(2,1)S(1)}, f32[16,4096]{1,0:T(8,128)S(1)}, s32[]{:T(128)}, s32[1,8]{1,0:T(1,128)S(1)}, /*index=5*/s32[3...) while((s32[]{:T(128)}, bf16[1536,512]{1,0:T(8,128)(2,1)S(1)}, ...), condition=%wide.region_2.3_spmd, body=%wide.region_0.2_spmd.sunk | while | flops 806617088 | bytes 21137560 | solution.py:41
  13.5 2.1 convolution_select_fusion.5
  15.6 1.5 convolution_select_fusion.6
  17.1 2.5 fusion.30
  19.5 2.2 collective-permute-start
  21.7 117.8 %reduce-scatter.2.cloned.1.call-done = f32[16,512]{1,0:T(8,128)} async-done(((f32[512,512]{1,0:T(8,128)}), f32[16,512]{1,0:T(8,128)}) %reduce-scatter.2.cloned.1.call-update) | async-done | bytes 32784 | tf_op jit(solution)/shard_map/while/body/eval_jaxpr/reduce_scatter | solution.py:35
  139.5 0.8 constant_dynamic-update-slice_fusion.2
  145.0 2.1 convolution_select_fusion.5
  147.1 1.5 convolution_select_fusion.6
  148.6 2.5 fusion.30
  151.1 116.8 %reduce-scatter.2.cloned.1.call-done = f32[16,512]{1,0:T(8,128)} async-done(((f32[512,512]{1,0:T(8,128)}), f32[16,512]{1,0:T(8,128)}) %reduce-scatter.2.cloned.1.call-update) | async-done | bytes 32784 | tf_op jit(solution)/shard_map/while/body/eval_jaxpr/reduce_scatter | solution.py:35
  268.0 0.8 constant_dynamic-update-slice_fusion.2
  273.4 2.1 convolution_select_fusion.5
  275.5 1.5 convolution_select_fusion.6
  277.0 2.5 fusion.30
  279.6 117.0 %reduce-scatter.2.cloned.1.call-done = f32[16,512]{1,0:T(8,128)} async-done(((f32[512,512]{1,0:T(8,128)}), f32[16,512]{1,0:T(8,128)}) %reduce-scatter.2.cloned.1.call-update) | async-done | bytes 32784 | tf_op jit(solution)/shard_map/while/body/eval_jaxpr/reduce_scatter | solution.py:35
  396.6 0.8 constant_dynamic-update-slice_fusion.2
  399.9 0.7 fusion.29
  402.1 2.1 convolution_select_fusion.5
  404.2 1.5 convolution_select_fusion.6
  405.7 2.5 fusion.30
  408.3 116.9 %reduce-scatter.2.cloned.1.call-done = f32[16,512]{1,0:T(8,128)} async-done(((f32[512,512]{1,0:T(8,128)}), f32[16,512]{1,0:T(8,128)}) %reduce-scatter.2.cloned.1.call-update) | async-done | bytes 32784 | tf_op jit(solution)/shard_map/while/body/eval_jaxpr/reduce_scatter | solution.py:35
  525.2 0.8 constant_dynamic-update-slice_fusion.2
  530.7 2.1 convolution_select_fusion.5
  532.8 1.5 convolution_select_fusion.6
  534.2 2.5 fusion.30
  536.9 116.9 %reduce-scatter.2.cloned.1.call-done = f32[16,512]{1,0:T(8,128)} async-done(((f32[512,512]{1,0:T(8,128)}), f32[16,512]{1,0:T(8,128)}) %reduce-scatter.2.cloned.1.call-update) | async-done | bytes 32784 | tf_op jit(solution)/shard_map/while/body/eval_jaxpr/reduce_scatter | solution.py:35
  653.8 0.8 constant_dynamic-update-slice_fusion.2
  659.2 2.1 convolution_select_fusion.5
  661.3 1.5 convolution_select_fusion.6
  662.8 2.5 fusion.30
  665.5 117.0 %reduce-scatter.2.cloned.1.call-done = f32[16,512]{1,0:T(8,128)} async-done(((f32[512,512]{1,0:T(8,128)}), f32[16,512]{1,0:T(8,128)}) %reduce-scatter.2.cloned.1.call-update) | async-done | bytes 32784 | tf_op jit(solution)/shard_map/while/body/eval_jaxpr/reduce_scatter | solution.py:35
  782.6 0.8 constant_dynamic-update-slice_fusion.2
  788.0 2.1 convolution_select_fusion.5
  790.1 1.5 convolution_select_fusion.6
  791.6 2.5 fusion.30
  794.5 116.7 %reduce-scatter.2.cloned.1.call-done = f32[16,512]{1,0:T(8,128)} async-done(((f32[512,512]{1,0:T(8,128)}), f32[16,512]{1,0:T(8,128)}) %reduce-scatter.2.cloned.1.call-update) | async-done | bytes 32784 | tf_op jit(solution)/shard_map/while/body/eval_jaxpr/reduce_scatter | solution.py:35
  911.2 0.8 constant_dynamic-update-slice_fusion.2
  916.7 2.1 convolution_select_fusion.5
  918.8 1.5 convolution_select_fusion.6
  920.3 2.5 fusion.30
  922.8 117.0 %reduce-scatter.2.cloned.1.call-done = f32[16,512]{1,0:T(8,128)} async-done(((f32[512,512]{1,0:T(8,128)}), f32[16,512]{1,0:T(8,128)}) %reduce-scatter.2.cloned.1.call-update) | async-done | bytes 32784 | tf_op jit(solution)/shard_map/while/body/eval_jaxpr/reduce_scatter | solution.py:35
  1039.9 0.8 constant_dynamic-update-slice_fusion.2
  1041.3 418.8 %all-gather.3.cloned.1.call-done = f32[1048576]{0:T(1024)} async-done(((f32[4096]{0:T(1024)}), f32[1048576]{0:T(1024)}) %all-gather.3.cloned.1.call-update) | async-done | bytes 4194320 | tf_op jit(solution)/shard_map/all_gather | solution.py:44
  1460.1 5.0 reshape.22
  1465.1 2.4 reduce_sum.19
  1467.5 0.7 multiply_divide_fusion
  (72 shorter events, 12.9 us)
Async XLA Ops:
  7.4 1.4 copy-start
  7.4 1.4 copy-start.1
  7.4 1.4 copy-start.2
  8.8 130.7 %reduce-scatter.2.cloned.1.call-start = ((), (), s32[]{:S(2)}) async-start(), calls=%async_computation.2 | async-start | bytes 1081344 | tf_op jit(solution)/shard_map/while/body/eval_jaxpr/reduce_scatter | solution.py:35
  19.5 120.8 %collective-permute-start = (bf16[1536,512]{1,0:T(8,128)(2,1)S(1)}, bf16[1536,512]{1,0:T(8,128)(2,1)S(1)}, u32[]{:S(2)}, u32[]{:S(2)}) collective-permute-start(bf16[1536,512]{1,0:T(8,128)(2,1)S(1)} %copy.10), channel_id=1, source_target_pairs={{0,32},{32,64},{64,96},{96,128},{128,160},{160,192},{192,224},{224... | collective-permute-start | bytes 4718600 | tf_op jit(solution)/shard_map/while/body/eval_jaxpr/ppermute | solution.py:9
  140.3 127.7 %reduce-scatter.2.cloned.1.call-start = ((), (), s32[]{:S(2)}) async-start(), calls=%async_computation.2 | async-start | bytes 1081344 | tf_op jit(solution)/shard_map/while/body/eval_jaxpr/reduce_scatter | solution.py:35
  151.0 117.7 %collective-permute-start = (bf16[1536,512]{1,0:T(8,128)(2,1)S(1)}, bf16[1536,512]{1,0:T(8,128)(2,1)S(1)}, u32[]{:S(2)}, u32[]{:S(2)}) collective-permute-start(bf16[1536,512]{1,0:T(8,128)(2,1)S(1)} %copy.10), channel_id=1, source_target_pairs={{0,32},{32,64},{64,96},{96,128},{128,160},{160,192},{192,224},{224... | collective-permute-start | bytes 4718600 | tf_op jit(solution)/shard_map/while/body/eval_jaxpr/ppermute | solution.py:9
  268.7 127.9 %reduce-scatter.2.cloned.1.call-start = ((), (), s32[]{:S(2)}) async-start(), calls=%async_computation.2 | async-start | bytes 1081344 | tf_op jit(solution)/shard_map/while/body/eval_jaxpr/reduce_scatter | solution.py:35
  279.5 117.9 %collective-permute-start = (bf16[1536,512]{1,0:T(8,128)(2,1)S(1)}, bf16[1536,512]{1,0:T(8,128)(2,1)S(1)}, u32[]{:S(2)}, u32[]{:S(2)}) collective-permute-start(bf16[1536,512]{1,0:T(8,128)(2,1)S(1)} %copy.10), channel_id=1, source_target_pairs={{0,32},{32,64},{64,96},{96,128},{128,160},{160,192},{192,224},{224... | collective-permute-start | bytes 4718600 | tf_op jit(solution)/shard_map/while/body/eval_jaxpr/ppermute | solution.py:9
  397.4 127.8 %reduce-scatter.2.cloned.1.call-start = ((), (), s32[]{:S(2)}) async-start(), calls=%async_computation.2 | async-start | bytes 1081344 | tf_op jit(solution)/shard_map/while/body/eval_jaxpr/reduce_scatter | solution.py:35
  408.2 117.8 %collective-permute-start = (bf16[1536,512]{1,0:T(8,128)(2,1)S(1)}, bf16[1536,512]{1,0:T(8,128)(2,1)S(1)}, u32[]{:S(2)}, u32[]{:S(2)}) collective-permute-start(bf16[1536,512]{1,0:T(8,128)(2,1)S(1)} %copy.10), channel_id=1, source_target_pairs={{0,32},{32,64},{64,96},{96,128},{128,160},{160,192},{192,224},{224... | collective-permute-start | bytes 4718600 | tf_op jit(solution)/shard_map/while/body/eval_jaxpr/ppermute | solution.py:9
  526.0 127.8 %reduce-scatter.2.cloned.1.call-start = ((), (), s32[]{:S(2)}) async-start(), calls=%async_computation.2 | async-start | bytes 1081344 | tf_op jit(solution)/shard_map/while/body/eval_jaxpr/reduce_scatter | solution.py:35
  536.7 117.8 %collective-permute-start = (bf16[1536,512]{1,0:T(8,128)(2,1)S(1)}, bf16[1536,512]{1,0:T(8,128)(2,1)S(1)}, u32[]{:S(2)}, u32[]{:S(2)}) collective-permute-start(bf16[1536,512]{1,0:T(8,128)(2,1)S(1)} %copy.10), channel_id=1, source_target_pairs={{0,32},{32,64},{64,96},{96,128},{128,160},{160,192},{192,224},{224... | collective-permute-start | bytes 4718600 | tf_op jit(solution)/shard_map/while/body/eval_jaxpr/ppermute | solution.py:9
  654.5 128.0 %reduce-scatter.2.cloned.1.call-start = ((), (), s32[]{:S(2)}) async-start(), calls=%async_computation.2 | async-start | bytes 1081344 | tf_op jit(solution)/shard_map/while/body/eval_jaxpr/reduce_scatter | solution.py:35
  665.3 118.0 %collective-permute-start = (bf16[1536,512]{1,0:T(8,128)(2,1)S(1)}, bf16[1536,512]{1,0:T(8,128)(2,1)S(1)}, u32[]{:S(2)}, u32[]{:S(2)}) collective-permute-start(bf16[1536,512]{1,0:T(8,128)(2,1)S(1)} %copy.10), channel_id=1, source_target_pairs={{0,32},{32,64},{64,96},{96,128},{128,160},{160,192},{192,224},{224... | collective-permute-start | bytes 4718600 | tf_op jit(solution)/shard_map/while/body/eval_jaxpr/ppermute | solution.py:9
  783.3 127.9 %reduce-scatter.2.cloned.1.call-start = ((), (), s32[]{:S(2)}) async-start(), calls=%async_computation.2 | async-start | bytes 1081344 | tf_op jit(solution)/shard_map/while/body/eval_jaxpr/reduce_scatter | solution.py:35
  794.1 117.9 %collective-permute-start = (bf16[1536,512]{1,0:T(8,128)(2,1)S(1)}, bf16[1536,512]{1,0:T(8,128)(2,1)S(1)}, u32[]{:S(2)}, u32[]{:S(2)}) collective-permute-start(bf16[1536,512]{1,0:T(8,128)(2,1)S(1)} %copy.10), channel_id=1, source_target_pairs={{0,32},{32,64},{64,96},{96,128},{128,160},{160,192},{192,224},{224... | collective-permute-start | bytes 4718600 | tf_op jit(solution)/shard_map/while/body/eval_jaxpr/ppermute | solution.py:9
  912.0 127.9 %reduce-scatter.2.cloned.1.call-start = ((), (), s32[]{:S(2)}) async-start(), calls=%async_computation.2 | async-start | bytes 1081344 | tf_op jit(solution)/shard_map/while/body/eval_jaxpr/reduce_scatter | solution.py:35
  922.7 117.9 %collective-permute-start = (bf16[1536,512]{1,0:T(8,128)(2,1)S(1)}, bf16[1536,512]{1,0:T(8,128)(2,1)S(1)}, u32[]{:S(2)}, u32[]{:S(2)}) collective-permute-start(bf16[1536,512]{1,0:T(8,128)(2,1)S(1)} %copy.10), channel_id=1, source_target_pairs={{0,32},{32,64},{64,96},{96,128},{128,160},{160,192},{192,224},{224... | collective-permute-start | bytes 4718600 | tf_op jit(solution)/shard_map/while/body/eval_jaxpr/ppermute | solution.py:9
  1040.6 419.5 %all-gather.3.cloned.1.call-start = ((), (), s32[]{:S(2)}) async-start(), calls=%async_computation.1 | async-start | bytes 4210688 | tf_op jit(solution)/shard_map/all_gather | solution.py:44
Sparse Core Ops, SparseCore 0:
  19.7 119.8 reduce-scatter.1
  151.2 116.7 reduce-scatter.1
  279.6 116.9 reduce-scatter.1
  408.3 116.8 reduce-scatter.1
  536.8 116.8 reduce-scatter.1
  665.4 117.1 reduce-scatter.1
  794.2 116.9 reduce-scatter.1
  922.9 116.9 reduce-scatter.1
Sparse Core Ops, SparseCore 1:
  1043.0 417.1 all-gather.2
